TPU v7x, 256 devices: a whole 4x4x8 slice. The times are simulated.
256 devices in a mesh: row: 8 (over x, z_hi), col: 8 (over z_lo, core), layer: 4 (over y).
Axes of the slice: x: 4, y: 4, z: 8 (z_hi: 2, z_lo: 4; z = z_hi * 4 + z_lo), core: 2. Of those that a mesh axis runs over, the one named last changes fastest.
Arguments:
- amplitudes: float32 [4096, 2048], P('row', ('col', 'layer')), may hold values from -6 to 6
- integrals: float32 [2048, 16384], P(('row', 'layer'), 'col'), may hold values from -0.125 to 0.125
Outputs:
- ladder: float32 [4096, 16384], P('row', ('col', 'layer'))
All inputs are finite; a program needn't handle non-finite values.
Results may differ from a plain program's by a relative error of at most 0.000082.
Values sent between devices are 32-bit elements; how exact they have to be, the bound alone decides.
A program may use at most 64 MiB of HBM per device.

v0:
```python
import jax
import jax.numpy as jnp
from jax import lax
from jax.sharding import PartitionSpec as P


def from_root(block, axis, holder):
    block = jnp.where(lax.axis_index(axis) == holder, block, jnp.zeros_like(block))
    return lax.psum(block, axis)


def summa(amp_panel, int_panel, step_count, first_step):
    spread = lax.axis_size("col") // lax.axis_size("row")
    partial_sum = jnp.zeros((amp_panel.shape[0], int_panel.shape[1]), jnp.float32)

    def one_turn(turn_at, total):
        block_at = first_step + turn_at
        amp_block = from_root(amp_panel, "col", block_at)
        int_block = from_root(int_panel, "row", block_at // spread)
        return total + jnp.dot(
            amp_block,
            int_block,
            precision=lax.Precision.HIGHEST,
            preferred_element_type=jnp.float32,
        )

    return lax.fori_loop(0, step_count, one_turn, partial_sum)


def contract(amp_panel, int_panel, step_count, first_step):
    return summa(amp_panel, int_panel, step_count, first_step)


def shards(amplitudes, integrals):
    cols_n = lax.axis_size("col")
    layers_n = lax.axis_size("layer")
    layer_at = lax.axis_index("layer")
    amp_panel = lax.all_gather(amplitudes, "layer", axis=1, tiled=True)
    int_panel = lax.all_gather(integrals, "layer", axis=0, tiled=True)
    step_count = cols_n // layers_n
    partial_sum = contract(amp_panel, int_panel, step_count, layer_at * step_count)
    product = lax.psum_scatter(partial_sum, "layer", scatter_dimension=1, tiled=True)
    return 0.5 * product


def solution(mesh):
    in_specs = (P("row", ("col", "layer")), P(("row", "layer"), "col"))
    out_specs = P("row", ("col", "layer"))
    return jax.shard_map(shards, mesh=mesh, in_specs=in_specs, out_specs=out_specs, check_vma=False)
```

profile of v0, /device:TPU:1, one launch (start us, length us, event | category | flops | bytes accessed | tf_op | source)
XLA Modules:
  0.0 660.9 jit_solution(806559248901591180)
XLA Ops:
  6.5 0.0 all-gather.2.cloned.1.call-start
  6.5 0.7 all-gather.2.cloned.1.call-update
  7.3 12.8 %all_gather.6 = f32[512,256]{0,1:T(8,128)S(1)} all-gather(f32[512,64]{0,1:T(8,128)} %param.4), channel_id=1, replica_groups=mesh['row'=8,'col'=8,'layer'=4] {'layer'}, dimensions={1}, use_global_device_ids=true | all-gather | bytes 655360 | tf_op jit(solution)/shard_map/all_gather | solution.py:38
  20.1 0.2 copy.4
  20.3 25.9 %all-gather.2.cloned.1.call-done = f32[256,2048]{1,0:T(8,128)} async-done(((f32[64,2048]{1,0:T(8,128)}), f32[256,2048]{1,0:T(8,128)}) %all-gather.2.cloned.1.call-update) | async-done | bytes 2097168 | tf_op jit(solution)/shard_map/all_gather | solution.py:39
  46.1 555.9 %while.16 = (s32[]{:T(128)}, f32[512,2048]{1,0:T(8,128)}, s32[]{:T(128)}, f32[512,256]{1,0:T(8,128)S(1)}, f32[256,2048]{1,0:T(8,128)}, /*index=5*/s32[]{:T(128)}, u32[]{:T(128)}, u32[]{:T(128)}, u32[]{:T(128)}, s32[]{:T(128)}) while((s32[]{:T(128)}, f32[512,2048]{1,0:T(8,128)}, s32[]{:T(128)}, f32[512,256]{1,0:T(8,128)S(1)}, ...), condition=%wide.region_3.4_spmd.clone, body=%wide.region_0.3_spmd.clone.sunk | while | flops 3224633344 | bytes 31981860 | solution.py:27
  46.1 0.0 all-reduce.3.cloned.1.call-start
  46.1 0.8 broadcast_select_fusion.4
  47.0 0.0 all-reduce.3.cloned.1.call-update
  47.0 0.0 all-reduce.5.cloned.1.call-start
  47.1 3.2 broadcast_select_fusion.5
  50.2 0.0 all-reduce.5.cloned.1.call-update
  50.3 68.8 %all-reduce.3.cloned.1.call-done = f32[512,256]{1,0:T(8,128)} async-done(((f32[512,256]{1,0:T(8,128)}), f32[512,256]{1,0:T(8,128)}) %all-reduce.3.cloned.1.call-update) | async-done | bytes 524304 | tf_op jit(solution)/shard_map/while/body/eval_jaxpr/psum | solution.py:9
  119.1 198.7 %all-reduce.5.cloned.1.call-done = f32[256,2048]{1,0:T(8,128)} async-done(((f32[256,2048]{1,0:T(8,128)}), f32[256,2048]{1,0:T(8,128)}) %all-reduce.5.cloned.1.call-update) | async-done | bytes 2097168 | tf_op jit(solution)/shard_map/while/body/eval_jaxpr/psum | solution.py:9
  317.8 7.4 %select_add_fusion.2 = f32[512,2048]{1,0:T(8,128)} fusion(f32[512,2048]{1,0:T(8,128)} %get-tuple-element.215, f32[512,256]{1,0:T(8,128)} %all-reduce.3.cloned.1.call-done, f32[256,2048]{1,0:T(8,128)} %all-reduce.5.cloned.1.call-done, pred[]{:T(512)S(6)} %compare.9), kind=kOutput, calls=%fused_computation.clone.1 | convolution fusion | flops 3223322624 | bytes 11010049 | tf_op jit(solution)/shard_map/while/body/eval_jaxpr/dot_general | solution.py:20
  325.2 0.0 all-reduce.3.cloned.1.call-start
  325.2 0.8 broadcast_select_fusion.4
  326.0 0.0 all-reduce.3.cloned.1.call-update
  326.0 0.0 all-reduce.5.cloned.1.call-start
  326.1 1.6 broadcast_select_fusion.5
  327.6 0.0 all-reduce.5.cloned.1.call-update
  327.7 67.2 %all-reduce.3.cloned.1.call-done = f32[512,256]{1,0:T(8,128)} async-done(((f32[512,256]{1,0:T(8,128)}), f32[512,256]{1,0:T(8,128)}) %all-reduce.3.cloned.1.call-update) | async-done | bytes 524304 | tf_op jit(solution)/shard_map/while/body/eval_jaxpr/psum | solution.py:9
  394.8 198.5 %all-reduce.5.cloned.1.call-done = f32[256,2048]{1,0:T(8,128)} async-done(((f32[256,2048]{1,0:T(8,128)}), f32[256,2048]{1,0:T(8,128)}) %all-reduce.5.cloned.1.call-update) | async-done | bytes 2097168 | tf_op jit(solution)/shard_map/while/body/eval_jaxpr/psum | solution.py:9
  593.4 8.6 %select_add_fusion.2 = f32[512,2048]{1,0:T(8,128)} fusion(f32[512,2048]{1,0:T(8,128)} %get-tuple-element.215, f32[512,256]{1,0:T(8,128)} %all-reduce.3.cloned.1.call-done, f32[256,2048]{1,0:T(8,128)} %all-reduce.5.cloned.1.call-done, pred[]{:T(512)S(6)} %compare.9), kind=kOutput, calls=%fused_computation.clone.1 | convolution fusion | flops 3223322624 | bytes 11010049 | tf_op jit(solution)/shard_map/while/body/eval_jaxpr/dot_general | solution.py:20
  602.0 0.0 reduce-scatter.2.cloned.1.call-start
  602.0 0.6 reduce-scatter.2.cloned.1.call-update
  602.6 49.1 %reduce-scatter.2.cloned.1.call-done = f32[512,512]{1,0:T(8,128)} async-done(((f32[512,2048]{1,0:T(8,128)}), f32[512,512]{1,0:T(8,128)}) %reduce-scatter.2.cloned.1.call-update) | async-done | bytes 1048592 | tf_op jit(solution)/shard_map/reduce_scatter | solution.py:42
  651.7 2.3 broadcast_multiply_fusion
  (1 shorter events, 0.0 us)
Async XLA Ops:
  6.5 39.6 %all-gather.2.cloned.1.call-start = ((), (), s32[]{:S(2)}) async-start(), calls=%async_computation.1 | async-start | bytes 2621440 | tf_op jit(solution)/shard_map/all_gather | solution.py:39
  46.1 72.9 %all-reduce.3.cloned.1.call-start = ((), (), s32[]{:S(2)}) async-start(), calls=%async_computation.3 | async-start | bytes 1048576 | tf_op jit(solution)/shard_map/while/body/eval_jaxpr/psum | solution.py:9
  47.0 270.8 %all-reduce.5.cloned.1.call-start = ((), (), s32[]{:S(2)}) async-start(), calls=%async_computation.4 | async-start | bytes 4194304 | tf_op jit(solution)/shard_map/while/body/eval_jaxpr/psum | solution.py:9
  325.2 69.7 %all-reduce.3.cloned.1.call-start = ((), (), s32[]{:S(2)}) async-start(), calls=%async_computation.3 | async-start | bytes 1048576 | tf_op jit(solution)/shard_map/while/body/eval_jaxpr/psum | solution.py:9
  326.0 267.4 %all-reduce.5.cloned.1.call-start = ((), (), s32[]{:S(2)}) async-start(), calls=%async_computation.4 | async-start | bytes 4194304 | tf_op jit(solution)/shard_map/while/body/eval_jaxpr/psum | solution.py:9
  602.0 49.7 %reduce-scatter.2.cloned.1.call-start = ((), (), s32[]{:S(2)}) async-start(), calls=%async_computation.2 | async-start | bytes 5242880 | tf_op jit(solution)/shard_map/reduce_scatter | solution.py:42
Sparse Core Ops, SparseCore 0:
  9.1 36.9 all-gather.1
  49.6 69.4 all-reduce.2
  121.7 195.9 all-reduce.4
  328.3 66.5 all-reduce.2
  397.4 195.9 all-reduce.4
  605.0 46.6 reduce-scatter.1
where the time goes:
time: 661 us
  waiting for transfers between devices  610 us (92%)
  matrix products  16 us (2%)
  between operations  13.4 us (2%)
  blocking collectives  12.8 us (2%)
  other arithmetic  8.69 us (1%)
    psum x4, waiting for transfers between devices, from_root(): return lax.psum(block, axis)  533 us
    reduce_scatter x1, waiting for transfers between devices, shards(): lax.psum_scatter(partial_sum, 'layer', scatter_dimension=1, tiled=True)  49.1 us
    all_gather x1, waiting for transfers between devices, shards(): int_panel = lax.all_gather(integrals, 'layer', axis=0, tiled=True)  25.9 us
    dot_general x2, matrix products, one_turn(): jnp.dot(amp_block, int_block, precision=lax.Precision.HIGHEST, preferred_...  16 us
  transfers between devices with their start and end apart: 6, of which 6 were waited for; matrix products, arithmetic and copies ran while one was open for 1% of the time, Pallas kernels for 0%

commit v1 on v0

--- a/solution.py
+++ b/solution.py
@@ -2,11 +2,13 @@
 import jax.numpy as jnp
 from jax import lax
 from jax.sharding import PartitionSpec as P
+from jax.lax import all_gather
 
 
 def from_root(block, axis, holder):
     block = jnp.where(lax.axis_index(axis) == holder, block, jnp.zeros_like(block))
-    return lax.psum(block, axis)
+    keep_up_the_teams = lambda ax_name, matrix: jnp.sum(all_gather(matrix, ax_name), axis=0)
+    return keep_up_the_teams(axis, block)
 
 
 def summa(amp_panel, int_panel, step_count, first_step):

time: 661 us -> 855 us (1.29)
  waiting for transfers between devices: 610 us -> 787 us
  other arithmetic: 8.69 us -> 29.2 us
    all_gather x0 -> x4, waiting for transfers between devices: none -> 712 us  [from_root(): all_gather(matrix, ax_name)]
    psum x4 -> x0, waiting for transfers between devices: 533 us -> none  [from_root(): return lax.psum(block, axis)]
    reduce_sum x0 -> x4, other arithmetic: none -> 20.6 us  [from_root(): jnp.sum(all_gather(matrix, ax_name), axis=0)]
where the time goes in v1:
time: 855 us
  waiting for transfers between devices  787 us (92%)
  other arithmetic  29.2 us (3%)
  between operations  13.4 us (2%)
  blocking collectives  12.8 us (1%)
  matrix products  12.2 us (1%)
    all_gather x4, waiting for transfers between devices, from_root(): all_gather(matrix, ax_name)  712 us
    reduce_scatter x1, waiting for transfers between devices, shards(): lax.psum_scatter(partial_sum, 'layer', scatter_dimension=1, tiled=True)  47.2 us
    all_gather x1, waiting for transfers between devices, shards(): int_panel = lax.all_gather(integrals, 'layer', axis=0, tiled=True)  25.9 us
    reduce_sum x4, other arithmetic, from_root(): jnp.sum(all_gather(matrix, ax_name), axis=0)  20.6 us
  transfers between devices with their start and end apart: 6, of which 6 were waited for; matrix products, arithmetic and copies ran while one was open for 1% of the time, Pallas kernels for 0%

profile of v1, /device:TPU:1, one launch (start us, length us, event | category | flops | bytes accessed | tf_op | source)
XLA Modules:
  0.0 854.8 jit_solution(3856589927848293111)
XLA Ops:
  6.5 0.0 all-gather.12.cloned.1.call-start
  6.5 0.7 all-gather.12.cloned.1.call-update
  7.3 12.8 %all_gather.32 = f32[512,256]{0,1:T(8,128)S(1)} all-gather(f32[512,64]{0,1:T(8,128)} %param.4), channel_id=1, replica_groups=mesh['row'=8,'col'=8,'layer'=4] {'layer'}, dimensions={1}, use_global_device_ids=true | all-gather | bytes 655360 | tf_op jit(solution)/shard_map/all_gather | solution.py:40
  20.1 0.2 copy.4
  20.3 25.9 %all-gather.12.cloned.1.call-done = f32[256,2048]{1,0:T(8,128)} async-done(((f32[64,2048]{1,0:T(8,128)}), f32[256,2048]{1,0:T(8,128)}) %all-gather.12.cloned.1.call-update) | async-done | bytes 2097168 | tf_op jit(solution)/shard_map/all_gather | solution.py:41
  46.1 751.7 %while.16 = (s32[]{:T(128)}, f32[512,2048]{1,0:T(8,128)}, s32[]{:T(128)}, f32[512,256]{1,0:T(8,128)S(1)}, f32[256,2048]{1,0:T(8,128)}, /*index=5*/s32[]{:T(128)}...) while((s32[]{:T(128)}, f32[512,2048]{1,0:T(8,128)}, s32[]{:T(128)}, ...), condition=%wide.region_3.4_spmd.clone, body=%wide.region_0.3_spmd.clone.sunk | while | flops 3228565504 | bytes 110625064 | solution.py:29
  46.1 0.0 all-gather.14.cloned.1.call-start
  46.1 0.8 broadcast_select_fusion.4
  47.0 0.0 all-gather.14.cloned.1.call-update
  47.0 0.0 all-gather.16.cloned.1.call-start
  47.1 3.1 broadcast_select_fusion.5
  50.2 0.0 all-gather.16.cloned.1.call-update
  50.2 51.2 %all-gather.14.cloned.1.call-done = f32[4096,256]{1,0:T(8,128)} async-done(((f32[512,256]{1,0:T(8,128)}), f32[4096,256]{1,0:T(8,128)}) %all-gather.14.cloned.1.call-update) | async-done | bytes 4194320 | tf_op jit(solution)/shard_map/while/body/eval_jaxpr/all_gather | solution.py:10
  101.4 2.5 reduce_sum.36
  103.9 306.9 %all-gather.16.cloned.1.call-done = f32[2048,2048]{1,0:T(8,128)} async-done(((f32[256,2048]{1,0:T(8,128)}), f32[2048,2048]{1,0:T(8,128)}) %all-gather.16.cloned.1.call-update) | async-done | bytes 16777232 | tf_op jit(solution)/shard_map/while/body/eval_jaxpr/all_gather | solution.py:10
  410.8 7.8 reduce_sum.37
  418.6 5.3 select_add_fusion.2
  423.9 0.0 all-gather.14.cloned.1.call-start
  423.9 0.8 broadcast_select_fusion.4
  424.7 0.0 all-gather.14.cloned.1.call-update
  424.8 0.0 all-gather.16.cloned.1.call-start
  424.8 1.5 broadcast_select_fusion.5
  426.3 0.0 all-gather.16.cloned.1.call-update
  426.4 47.6 %all-gather.14.cloned.1.call-done = f32[4096,256]{1,0:T(8,128)} async-done(((f32[512,256]{1,0:T(8,128)}), f32[4096,256]{1,0:T(8,128)}) %all-gather.14.cloned.1.call-update) | async-done | bytes 4194320 | tf_op jit(solution)/shard_map/while/body/eval_jaxpr/all_gather | solution.py:10
  474.0 2.5 reduce_sum.36
  476.5 306.7 %all-gather.16.cloned.1.call-done = f32[2048,2048]{1,0:T(8,128)} async-done(((f32[256,2048]{1,0:T(8,128)}), f32[2048,2048]{1,0:T(8,128)}) %all-gather.16.cloned.1.call-update) | async-done | bytes 16777232 | tf_op jit(solution)/shard_map/while/body/eval_jaxpr/all_gather | solution.py:10
  783.2 7.8 reduce_sum.37
  791.0 6.9 select_add_fusion.2
  797.9 0.0 reduce-scatter.2.cloned.1.call-start
  797.9 0.6 reduce-scatter.2.cloned.1.call-update
  798.5 47.2 %reduce-scatter.2.cloned.1.call-done = f32[512,512]{1,0:T(8,128)} async-done(((f32[512,2048]{1,0:T(8,128)}), f32[512,512]{1,0:T(8,128)}) %reduce-scatter.2.cloned.1.call-update) | async-done | bytes 1048592 | tf_op jit(solution)/shard_map/reduce_scatter | solution.py:44
  845.7 2.3 broadcast_multiply_fusion
  (1 shorter events, 0.0 us)
Async XLA Ops:
  6.5 39.6 %all-gather.12.cloned.1.call-start = ((), (), s32[]{:S(2)}) async-start(), calls=%async_computation.1 | async-start | bytes 2621440 | tf_op jit(solution)/shard_map/all_gather | solution.py:41
  46.1 55.3 %all-gather.14.cloned.1.call-start = ((), (), s32[]{:S(2)}) async-start(), calls=%async_computation.3 | async-start | bytes 4718592 | tf_op jit(solution)/shard_map/while/body/eval_jaxpr/all_gather | solution.py:10
  47.0 363.8 %all-gather.16.cloned.1.call-start = ((), (), s32[]{:S(2)}) async-start(), calls=%async_computation.4 | async-start | bytes 18874368 | tf_op jit(solution)/shard_map/while/body/eval_jaxpr/all_gather | solution.py:10
  423.9 50.1 %all-gather.14.cloned.1.call-start = ((), (), s32[]{:S(2)}) async-start(), calls=%async_computation.3 | async-start | bytes 4718592 | tf_op jit(solution)/shard_map/while/body/eval_jaxpr/all_gather | solution.py:10
  424.8 358.5 %all-gather.16.cloned.1.call-start = ((), (), s32[]{:S(2)}) async-start(), calls=%async_computation.4 | async-start | bytes 18874368 | tf_op jit(solution)/shard_map/while/body/eval_jaxpr/all_gather | solution.py:10
  797.9 47.8 %reduce-scatter.2.cloned.1.call-start = ((), (), s32[]{:S(2)}) async-start(), calls=%async_computation.2 | async-start | bytes 5242880 | tf_op jit(solution)/shard_map/reduce_scatter | solution.py:44
Sparse Core Ops, SparseCore 0:
  9.1 36.9 all-gather.11
  48.7 52.6 all-gather.13
  104.0 306.7 all-gather.15
  426.2 47.8 all-gather.13
  476.5 306.7 all-gather.15
  800.9 44.6 reduce-scatter.1
